TPU v7x, 512 devices: a whole 4x8x8 slice. The times are simulated.
512 devices in a mesh: lat: 16 (over z, x_hi), lon: 32 (over y, x_lo, core).
Axes of the slice: x: 4 (x_hi: 2, x_lo: 2; x = x_hi * 2 + x_lo), y: 8, z: 8, core: 2. Of those that a mesh axis runs over, the one named last changes fastest.
Arguments:
- frame: bfloat16 [256, 512, 256], P('lat', 'lon'), may hold values from -64 to 64
- weight_qkv: bfloat16 [256, 768], replicated, may hold values from -0.375 to 0.375
- weight_proj: bfloat16 [256, 256], replicated, may hold values from -0.375 to 0.375
- gain_attn: float32 [256], replicated, may hold values from 0.5 to 1.5
- weight_up: bfloat16 [256, 1024], replicated, may hold values from -0.375 to 0.375
- weight_down: bfloat16 [1024, 256], replicated, may hold values from -0.1875 to 0.1875
- gain_mlp: float32 [256], replicated, may hold values from 0.5 to 1.5
- cotangent: bfloat16 [256, 512, 256], P('lat', 'lon'), may hold values from -6 to 6
Outputs:
- block_out: bfloat16 [256, 512, 256], P('lat', 'lon')
- grad_frame: bfloat16 [256, 512, 256], P('lat', 'lon')
- grad_qkv: bfloat16 [256, 768], replicated
- grad_proj: bfloat16 [256, 256], replicated
- grad_up: bfloat16 [256, 1024], replicated
- grad_down: bfloat16 [1024, 256], replicated
- grad_gain_attn: float32 [256], replicated
- grad_gain_mlp: float32 [256], replicated
All inputs are finite; a program needn't handle non-finite values.
Results may differ from a plain program's by a relative error of at most 0.012.
The roundings to bfloat16 on the way count: a program that leaves them out, or rounds other values in their place, can miss the bound.
Values may be sent and summed in bfloat16 or wider, within the bound.
No kernel may reach another device: no remote copies, remote signals or barrier semaphores. Data moves between devices by JAX's collectives and lax.ppermute only.
A program may use at most 128 MiB of HBM per device.

v0:
```python
import jax
import jax.numpy as jnp
from jax import lax
from jax.sharding import PartitionSpec as P

HEADS = 8
RADIUS = 6
epsilon = 1e-06
cubic_term = 0.044715
gelu_root = 0.7978845608028654
negative_big = -1e30


def padded_2(x, sides, width, wrap):
    for axis, dim in sides:
        devices, length = (lax.axis_size(axis), x.shape[dim])
        up = [(i, (i + 1) % devices) for i in range(devices if wrap else devices - 1)]
        down = [(j, i) for i, j in up]
        last = lax.slice_in_dim(x, length - width, length, axis=dim)
        first = lax.slice_in_dim(x, 0, width, axis=dim)
        before = lax.ppermute(last, axis, up)
        after = lax.ppermute(first, axis, down)
        x = jnp.concatenate([before, x, after], axis=dim)
    return x


def gelu_pair(upward):
    tangent = jnp.tanh(gelu_root * (upward + cubic_term * upward * upward * upward))
    activated = 0.5 * upward * (1.0 + tangent)
    derivative = 0.5 * (1.0 + tangent) + 0.5 * upward * (1.0 - tangent * tangent) * gelu_root * (
        1.0 + 3.0 * cubic_term * upward * upward
    )
    return (activated, derivative)


def rms_factor(field):
    return lax.rsqrt(jnp.mean(field * field, axis=-1, keepdims=True) + epsilon)


def norm_backward(incoming, field, factor):
    mean_term = jnp.mean(incoming * field, axis=-1, keepdims=True)
    return factor * (incoming - field * factor * factor * mean_term)


def contract_rows(left, right):
    return lax.dot_general(
        left, right, (((0,), (0,)), ((), ())), preferred_element_type=jnp.float32
    )


def contract_cols(left, right):
    return lax.dot_general(
        left, right, (((1,), (1,)), ((), ())), preferred_element_type=jnp.float32
    )


def row_strips(padded, rows, span):
    return jnp.stack(
        [lax.slice_in_dim(padded, offset, offset + rows, axis=0) for offset in range(span)], axis=1
    )


def unstrip(strip_sum, rows, span):
    total = jnp.zeros((rows + span - 1,) + strip_sum.shape[2:], strip_sum.dtype)
    for offset in range(span):
        total = total.at[offset : offset + rows].add(strip_sum[:, offset])
    return total


def fold_rims(field, axis, length, radius):
    middle = lax.slice_in_dim(field, 2 * radius, 2 * radius + length, axis=axis)
    front = lax.slice_in_dim(field, 0, radius, axis=axis)
    back = lax.slice_in_dim(field, length + 3 * radius, length + 4 * radius, axis=axis)
    widths_front = [(0, 0)] * field.ndim
    widths_front[axis] = (0, length - radius)
    widths_back = [(0, 0)] * field.ndim
    widths_back[axis] = (length - radius, 0)
    return middle + jnp.pad(front, widths_front) + jnp.pad(back, widths_back)


def band_strips(padded, rows, span, heads):
    strips = row_strips(padded, rows, span)
    return strips.reshape(rows, span * padded.shape[1], heads, padded.shape[2] // heads)


def on_device(
    frame, weight_qkv, weight_proj, gain_attn, weight_up, weight_down, gain_mlp, cotangent
):
    lat_rows, lon_cols, width = frame.shape
    heads = HEADS
    head_size = width // heads
    radius = RADIUS
    span = 2 * radius + 1
    head_scale = head_size ** (-0.5)
    pad_rows = lat_rows + 2 * radius
    pad_cols = lon_cols + 2 * radius
    band = span * pad_cols
    local_tokens = lat_rows * lon_cols
    lat_total = lat_rows * lax.axis_size("lat")
    tokens_all = lat_total * lon_cols * lax.axis_size("lon")
    grad_scale = tokens_all ** (-0.5)
    lat_first = lax.axis_index("lat") * lat_rows
    row_global = lat_first + jnp.arange(lat_rows)[:, None] + jnp.arange(span)[None, :] - radius
    row_ok = (row_global >= 0) & (row_global < lat_total)
    col_gap = jnp.arange(pad_cols)[None, :] - radius - jnp.arange(lon_cols)[:, None]
    near = jnp.abs(col_gap) <= radius
    valid = (row_ok[:, None, :, None] & near[None, :, None, :]).reshape(lat_rows, 1, lon_cols, band)
    flat = frame.reshape(local_tokens, width)
    projected = jnp.dot(flat, weight_qkv, preferred_element_type=jnp.float32).astype(jnp.bfloat16)
    queries = projected[:, :width]
    pairs = projected[:, width:].reshape(lat_rows, lon_cols, 2 * width)
    widened = padded_2(pairs, (("lon", 1),), radius, True)
    margined = padded_2(widened, (("lat", 0),), radius, False)
    pair_pad = margined.reshape(-1, 2 * width)
    queries4 = queries.reshape(lat_rows, lon_cols, heads, head_size)
    keys_pad = pair_pad[:, :width].reshape(pad_rows, pad_cols, width)
    values_pad = pair_pad[:, width:].reshape(pad_rows, pad_cols, width)
    key_strip = band_strips(keys_pad, lat_rows, span, heads)
    value_strip = band_strips(values_pad, lat_rows, span, heads)
    scores = (
        jnp.einsum("ichd,inhd->ihcn", queries4, key_strip, preferred_element_type=jnp.float32)
        * head_scale
    )
    scores = jnp.where(valid, scores, negative_big)
    peak = jnp.max(scores, axis=3, keepdims=True)
    expo = jnp.exp(scores - peak)
    total = jnp.sum(expo, axis=3, keepdims=True)
    probs = expo / total
    probs_bf = probs.astype(jnp.bfloat16)
    attended = (
        jnp.einsum("ihcn,inhd->ichd", probs_bf, value_strip, preferred_element_type=jnp.float32)
        .astype(jnp.bfloat16)
        .reshape(local_tokens, width)
    )
    proj = jnp.dot(attended, weight_proj, preferred_element_type=jnp.float32)
    factor_one = rms_factor(proj)
    mid = (flat.astype(jnp.float32) + proj * factor_one * gain_attn).astype(jnp.bfloat16)
    upward = jnp.dot(mid, weight_up, preferred_element_type=jnp.float32)
    activated, derivative = gelu_pair(upward)
    hidden = activated.astype(jnp.bfloat16)
    downward = jnp.dot(hidden, weight_down, preferred_element_type=jnp.float32)
    factor_two = rms_factor(downward)
    block_out = (mid.astype(jnp.float32) + downward * factor_two * gain_mlp).astype(jnp.bfloat16)
    incoming = cotangent.reshape(local_tokens, width).astype(jnp.float32)
    local_gain_mlp = jnp.sum(incoming * downward * factor_two, axis=0)
    d_down = norm_backward(incoming * gain_mlp, downward, factor_two).astype(jnp.bfloat16)
    local_down = contract_rows(hidden, d_down)
    d_up = (contract_cols(d_down, weight_down) * derivative).astype(jnp.bfloat16)
    local_up = contract_rows(mid, d_up)
    d_mid = incoming + contract_cols(d_up, weight_up)
    local_gain_attn = jnp.sum(d_mid * proj * factor_one, axis=0)
    d_proj = norm_backward(d_mid * gain_attn, proj, factor_one).astype(jnp.bfloat16)
    local_proj = contract_rows(attended, d_proj)
    d_attended = contract_cols(d_proj, weight_proj).astype(jnp.bfloat16)
    d_attended4 = d_attended.reshape(lat_rows, lon_cols, heads, head_size)
    d_probs = jnp.einsum(
        "ichd,inhd->ihcn", d_attended4, value_strip, preferred_element_type=jnp.float32
    )
    d_weighted = jnp.sum(probs * d_probs, axis=3, keepdims=True)
    d_scores = (probs * (d_probs - d_weighted) * head_scale).astype(jnp.bfloat16)
    d_queries = jnp.einsum(
        "ihcn,inhd->ichd", d_scores, key_strip, preferred_element_type=jnp.float32
    ).reshape(local_tokens, width)
    key_terms = jnp.einsum(
        "ihcn,ichd->inhd", d_scores, queries4, preferred_element_type=jnp.float32
    ).reshape(lat_rows, span, pad_cols, width)
    value_terms = jnp.einsum(
        "ihcn,ichd->inhd", probs_bf, d_attended4, preferred_element_type=jnp.float32
    ).reshape(lat_rows, span, pad_cols, width)
    pair_grads = unstrip(jnp.concatenate([key_terms, value_terms], axis=3), lat_rows, span)
    widened_grads = padded_2(pair_grads.astype(jnp.bfloat16), (("lon", 1),), radius, True).astype(
        pair_grads.dtype
    )
    margined_grads = padded_2(
        widened_grads.astype(jnp.bfloat16), (("lat", 0),), radius, False
    ).astype(widened_grads.dtype)
    owned = fold_rims(fold_rims(margined_grads, 0, lat_rows, radius), 1, lon_cols, radius).reshape(
        local_tokens, 2 * width
    )
    d_projected = jnp.concatenate([d_queries, owned], axis=1).astype(jnp.bfloat16)
    local_qkv = contract_rows(flat, d_projected)
    grad_frame = (d_mid + contract_cols(d_projected, weight_qkv)).astype(jnp.bfloat16)
    sum_qkv, sum_proj, sum_up, sum_down, sum_gain_attn, sum_gain_mlp = lax.psum(
        (local_qkv, local_proj, local_up, local_down, local_gain_attn, local_gain_mlp),
        ("lat", "lon"),
    )
    return (
        block_out.reshape(lat_rows, lon_cols, width),
        grad_frame.reshape(lat_rows, lon_cols, width),
        (sum_qkv * grad_scale).astype(jnp.bfloat16),
        (sum_proj * grad_scale).astype(jnp.bfloat16),
        (sum_up * grad_scale).astype(jnp.bfloat16),
        (sum_down * grad_scale).astype(jnp.bfloat16),
        sum_gain_attn * grad_scale,
        sum_gain_mlp * grad_scale,
    )


def solution(mesh):
    return jax.shard_map(
        on_device,
        mesh=mesh,
        in_specs=(P("lat", "lon", None), P(), P(), P(), P(), P(), P(), P("lat", "lon", None)),
        out_specs=(P("lat", "lon", None), P("lat", "lon", None), P(), P(), P(), P(), P(), P()),
        check_vma=False,
    )
```

profile of v0, /device:TPU:17, one launch (start us, length us, event | category | flops | bytes accessed | tf_op | source)
XLA Modules:
  0.0 695.6 jit_solution(14059497985502001922)
XLA Ops:
  8.7 3.7 collective-permute-start
  12.4 1.9 collective-permute-start.1
  15.1 3.6 collective-permute-done.1
  18.8 4.4 collective-permute-start.2
  25.2 2.3 collective-permute-done.2
  27.4 5.3 collective-permute-done.3
  34.0 2.1 fusion.75
  38.9 1.7 stack.109
  47.4 1.7 stack.104
  50.8 1.7 stack.102
  52.4 1.7 stack.101
  55.8 1.7 stack.99
  64.5 1.8 constant_dynamic-update-slice_fusion.25
  79.8 18.8 %copy.50 = bf16[16,13,28,256]{2,1,3,0:T(8,128)(2,1)} copy(bf16[16,13,28,256]{3,2,0,1:T(8,128)(2,1)} %constant_dynamic-update-slice_fusion.13) | data formatting | bytes 5963776 | tf_op jit(solution)/shard_map/reshape | solution.py:83
  98.6 21.2 %reshape.626 = bf16[16,364,8,32]{1,3,2,0:T(8,128)(2,1)} reshape(bf16[16,13,28,256]{2,1,3,0:T(8,128)(2,1)} %copy.50) | data formatting | bytes 5963776 | tf_op jit(solution)/shard_map/reshape | solution.py:83
  128.6 18.8 %copy.49 = bf16[16,13,28,256]{2,1,3,0:T(8,128)(2,1)} copy(bf16[16,13,28,256]{3,2,0,1:T(8,128)(2,1)} %constant_dynamic-update-slice_fusion) | data formatting | bytes 5963776 | tf_op jit(solution)/shard_map/reshape | solution.py:83
  147.4 21.2 %reshape.625 = bf16[16,364,8,32]{1,3,2,0:T(8,128)(2,1)} reshape(bf16[16,13,28,256]{2,1,3,0:T(8,128)(2,1)} %copy.49) | data formatting | bytes 5963776 | tf_op jit(solution)/shard_map/reshape | solution.py:83
  168.6 2.6 fusion.52
  171.2 3.8 fusion.78
  182.0 4.3 fusion.49
  186.3 17.5 %fusion.20 = bf16[16,16,8,32]{3,1,2,0:T(8,128)(2,1)} fusion(bf16[16,364,8,32]{1,3,2,0:T(8,128)(2,1)} %reshape.626, f32[16,8,16,364]{3,2,1,0:T(8,128)} %fusion.49, f32[16,8,16,364]{3,2,1,0:T(8,128)} %copy-done.5, f32[16,8,16]{2,1,0:T(8,128)S(1)} %get-tuple-element.226), kind=kOutput, calls=%fused_computation.27 | convolution fusion | flops 52996460 | bytes 9084928 | tf_op jit(solution)/shard_map/ihcn,inhd->ichd/dot_general | solution.py:161
  203.8 17.6 %convolution_bitcast_fusion.1 = f32[16,364,8,32]{1,3,2,0:T(8,128)} fusion(f32[16,8,16,364]{3,2,1,0:T(8,128)} %fusion.49, bf16[16,16,8,32]{3,2,1,0:T(8,128)(2,1)S(1)} %reshape.602, f32[16,8,16,364]{3,2,1,0:T(8,128)} %copy-done.5, f32[16,8,16]{2,1,0:T(8,128)S(1)} %get-tuple-element.226), kind=kOutput, calls=%fused_computation.8 | convolution fusion | flops 52930924 | bytes 12066816 | tf_op jit(solution)/shard_map/ihcn,ichd->inhd/dot_general | solution.py:164
  221.3 5.6 convolution_bitcast_fusion
  226.9 20.3 %copy.46 = f32[16,364,8,32]{3,2,0,1:T(8,128)} copy(f32[16,364,8,32]{1,3,2,0:T(8,128)} %convolution_bitcast_fusion) | data formatting | bytes 11927552 | tf_op jit(solution)/shard_map/ihcn,ichd->inhd/transpose | solution.py:167
  247.3 16.9 %reshape.609 = f32[16,13,28,256]{3,0,2,1:T(8,128)} reshape(f32[16,364,8,32]{3,2,0,1:T(8,128)} %copy.46) | data formatting | bytes 11927552 | tf_op jit(solution)/shard_map/reshape | solution.py:169
  264.2 20.3 %copy.44 = f32[16,364,8,32]{3,2,0,1:T(8,128)} copy(f32[16,364,8,32]{1,3,2,0:T(8,128)} %convolution_bitcast_fusion.1) | data formatting | bytes 11927552 | tf_op jit(solution)/shard_map/ihcn,ichd->inhd/transpose | solution.py:164
  284.5 16.8 %reshape.608 = f32[16,13,28,256]{3,0,2,1:T(8,128)} reshape(f32[16,364,8,32]{3,2,0,1:T(8,128)} %copy.44) | data formatting | bytes 11927552 | tf_op jit(solution)/shard_map/reshape | solution.py:166
  301.3 3.8 constant_dynamic-update-slice_fusion.27
  307.7 4.1 copy-done.2
  312.0 2.2 scatter-add.45
  315.6 2.2 scatter-add.46
  319.3 2.2 scatter-add.49
  322.9 2.2 scatter-add.50
  326.5 2.2 scatter-add.51
  330.2 2.2 scatter-add.54
  333.8 2.2 scatter-add.55
  338.8 2.5 scatter-add.59
  342.8 2.5 scatter-add.60
  346.7 2.5 scatter-add.61
  350.6 2.5 scatter-add.64
  353.3 2.1 collective-permute-start.4
  355.3 3.2 collective-permute-start.5
  360.1 3.7 collective-permute-done.5
  364.8 5.1 collective-permute-start.6
  374.2 9.6 %collective-permute-done.6 = bf16[6,40,512]{2,0,1:T(8,128)(2,1)S(1)} collective-permute-done((bf16[6,40,512]{2,0,1:T(8,128)(2,1)}, bf16[6,40,512]{2,0,1:T(8,128)(2,1)S(1)}, u32[]{:S(2)}, u32[]{:S(2)}) %collective-permute-start.6) | collective-permute-done | bytes 245792 | tf_op jit(solution)/shard_map/ppermute | solution.py:21
  386.7 106.6 %all-reduce.3 = (f32[256]{0:T(256)S(1)}, f32[256]{0:T(256)S(1)}) all-reduce(f32[256]{0:T(256)S(1)} %get-tuple-element.180, f32[256]{0:T(256)S(1)} %get-tuple-element.182), channel_id=1, replica_groups=mesh['lat'=16,'lon'=32] {'lat','lon'}, use_global_device_ids=true, to_apply=%region_12.13 | all-reduce | flops 512 | bytes 4096 | tf_op jit(solution)/shard_map/psum | solution.py:183
  494.9 186.8 %all-reduce.7.cloned.1.call-done = (f32[256,768]{0,1:T(8,128)}, f32[256,256]{1,0:T(8,128)}, f32[256,1024]{1,0:T(8,128)}, f32[1024,256]{1,0:T(8,128)}) async-done(((f32[256,768]{0,1:T(8,128)}, f32[256,256]{1,0:T(8,128)}, f32[256,1024]{1,0:T(8,128)}, f32[1024,256]{1,0:T(8,128)}), (f32[256,768]{0,1:T(8,128)}, f32[256,256]{1,0:T(8,128)}, f32[256,1024]{1,0:T(8,128)}, ...) | async-done | bytes 3145744 | tf_op jit(solution)/shard_map/psum | solution.py:183
  685.5 2.1 multiply_convert_fusion.2
  (210 shorter events, 88.8 us)
Async XLA Ops:
  7.2 170.5 %copy-start = (bf16[256,1024]{1,0:T(8,128)(2,1)S(1)}, bf16[256,1024]{1,0:T(8,128)(2,1)}, u32[]{:S(2)}) copy-start(bf16[256,1024]{1,0:T(8,128)(2,1)} %param.38) | copy-start | bytes 1572868
  7.2 674.5 %all-reduce.7.cloned.1.call-start = ((), (), s32[]{:S(2)}) async-start(), calls=%async_computation | async-start | bytes 6291456 | tf_op jit(solution)/shard_map/psum | solution.py:183
  8.7 6.4 collective-permute-start
  12.4 6.3 collective-permute-start.1
  18.8 8.6 %collective-permute-start.2 = (bf16[6,28,512]{2,1,0:T(8,128)(2,1)S(1)}, bf16[6,28,512]{2,1,0:T(8,128)(2,1)S(1)}, u32[]{:S(2)}, u32[]{:S(2)}) collective-permute-start(bf16[6,28,512]{2,1,0:T(8,128)(2,1)S(1)} %get-tuple-element.220), channel_id=1, source_target_pairs={{0,32},{32,64},{64,96},{96,128},{128,160},{160,192},{192,224},{224... | collective-permute-start | bytes 516104 | tf_op jit(solution)/shard_map/ppermute | solution.py:21
  23.2 9.6 %collective-permute-start.3 = (bf16[6,28,512]{2,1,0:T(8,128)(2,1)S(1)}, bf16[6,28,512]{2,1,0:T(8,128)(2,1)S(1)}, u32[]{:S(2)}, u32[]{:S(2)}) collective-permute-start(bf16[6,28,512]{2,1,0:T(8,128)(2,1)S(1)} %get-tuple-element.221), channel_id=1, source_target_pairs={{32,0},{64,32},{96,64},{128,96},{160,128},{192,160},{224,192},{256... | collective-permute-start | bytes 516104 | tf_op jit(solution)/shard_map/ppermute | solution.py:22
  37.1 1.0 copy-start.32
  38.1 19.4 %copy-start.31 = (bf16[448,256]{1,0:T(8,128)(2,1)S(1)}, bf16[448,256]{1,0:T(8,128)(2,1)}, u32[]{:S(2)}) copy-start(bf16[448,256]{1,0:T(8,128)(2,1)} %get-tuple-element.206) | copy-start | bytes 688132
  38.1 20.1 %copy-start.30 = (bf16[448,256]{1,0:T(8,128)(2,1)S(1)}, bf16[448,256]{1,0:T(8,128)(2,1)}, u32[]{:S(2)}) copy-start(bf16[448,256]{1,0:T(8,128)(2,1)} %get-tuple-element.207) | copy-start | bytes 688132
  38.9 19.4 %copy-start.29 = (bf16[448,256]{1,0:T(8,128)(2,1)S(1)}, bf16[448,256]{1,0:T(8,128)(2,1)}, u32[]{:S(2)}) copy-start(bf16[448,256]{1,0:T(8,128)(2,1)} %get-tuple-element.208) | copy-start | bytes 688132
  64.5 10.2 %copy-start.26 = (bf16[16,1,28,256]{3,2,0,1:T(8,128)(2,1)S(1)}, bf16[16,1,28,256]{3,2,0,1:T(8,128)(2,1)}, u32[]{:S(2)}) copy-start(bf16[16,1,28,256]{3,2,0,1:T(8,128)(2,1)} %stack.104) | copy-start | bytes 688132
  64.5 10.9 %copy-start.25 = (bf16[16,1,28,256]{3,2,0,1:T(8,128)(2,1)S(1)}, bf16[16,1,28,256]{3,2,0,1:T(8,128)(2,1)}, u32[]{:S(2)}) copy-start(bf16[16,1,28,256]{3,2,0,1:T(8,128)(2,1)} %stack.105) | copy-start | bytes 688132
  64.5 11.7 %copy-start.24 = (bf16[16,1,28,256]{3,2,0,1:T(8,128)(2,1)S(1)}, bf16[16,1,28,256]{3,2,0,1:T(8,128)(2,1)}, u32[]{:S(2)}) copy-start(bf16[16,1,28,256]{3,2,0,1:T(8,128)(2,1)} %stack.106) | copy-start | bytes 688132
  64.5 12.4 %copy-start.23 = (bf16[16,1,28,256]{3,2,0,1:T(8,128)(2,1)S(1)}, bf16[16,1,28,256]{3,2,0,1:T(8,128)(2,1)}, u32[]{:S(2)}) copy-start(bf16[16,1,28,256]{3,2,0,1:T(8,128)(2,1)} %stack.107) | copy-start | bytes 688132
  64.5 13.1 %copy-start.21 = (bf16[16,1,28,256]{3,2,0,1:T(8,128)(2,1)S(1)}, bf16[16,1,28,256]{3,2,0,1:T(8,128)(2,1)}, u32[]{:S(2)}) copy-start(bf16[16,1,28,256]{3,2,0,1:T(8,128)(2,1)} %stack.108) | copy-start | bytes 688132
  64.5 13.9 %copy-start.19 = (bf16[16,1,28,256]{3,2,0,1:T(8,128)(2,1)S(1)}, bf16[16,1,28,256]{3,2,0,1:T(8,128)(2,1)}, u32[]{:S(2)}) copy-start(bf16[16,1,28,256]{3,2,0,1:T(8,128)(2,1)} %stack.109) | copy-start | bytes 688132
  64.5 14.6 %copy-start.17 = (bf16[16,1,28,256]{3,2,0,1:T(8,128)(2,1)S(1)}, bf16[16,1,28,256]{3,2,0,1:T(8,128)(2,1)}, u32[]{:S(2)}) copy-start(bf16[16,1,28,256]{3,2,0,1:T(8,128)(2,1)} %stack.110) | copy-start | bytes 688132
  119.8 4.3 copy-start.22
  119.8 5.1 copy-start.20
  119.8 5.8 copy-start.18
  168.6 2.6 copy-start.38
  171.2 3.8 copy-start.4
  175.0 1.6 copy-start.5
  175.0 2.1 copy-start.34
  175.1 2.4 copy-start.8
  175.1 2.4 copy-start.39
  176.7 1.3 copy-start.42
  176.8 1.7 copy-start.13
  176.8 1.7 copy-start.40
  177.2 1.5 copy-start.11
  178.0 2.4 copy-start.27
  181.5 4.7 copy-start.9
  301.3 4.4 copy-start.3
  307.4 4.4 copy-start.2
  353.1 5.4 copy-start.28
  353.1 5.4 copy-start.37
  353.2 18.2 %copy-start.7 = (bf16[256,1024]{1,0:T(8,128)(2,1)S(1)}, bf16[256,1024]{1,0:T(8,128)(2,1)}, u32[]{:S(2)}) copy-start(bf16[256,1024]{1,0:T(8,128)(2,1)} %copy-done.6) | copy-start | bytes 1572868
  353.3 6.8 collective-permute-start.4
  355.3 17.4 %copy-start.33 = (bf16[16,16,8,32]{3,1,2,0:T(8,128)(2,1)S(1)}, bf16[16,16,8,32]{3,1,2,0:T(8,128)(2,1)}, u32[]{:S(2)}) copy-start(bf16[16,16,8,32]{3,1,2,0:T(8,128)(2,1)} %fusion.20) | copy-start | bytes 393220
  355.3 8.5 %collective-permute-start.5 = (bf16[28,6,512]{2,0,1:T(8,128)(2,1)S(1)}, bf16[28,6,512]{2,0,1:T(8,128)(2,1)S(1)}, u32[]{:S(2)}, u32[]{:S(2)}) collective-permute-start(bf16[28,6,512]{2,0,1:T(8,128)(2,1)S(1)} %get-tuple-element.193), channel_id=1, source_target_pairs={{1,0},{2,1},{3,2},{4,3},{5,4},{6,5},{7,6},{8,7},{9,8},{10,9},{11,1... | collective-permute-start | bytes 516104 | tf_op jit(solution)/shard_map/ppermute | solution.py:22
  360.1 13.1 %copy-start.10 = (bf16[256,256]{1,0:T(8,128)(2,1)S(1)}, bf16[256,256]{1,0:T(8,128)(2,1)}, u32[]{:S(2)}) copy-start(bf16[256,256]{1,0:T(8,128)(2,1)} %copy-done.9) | copy-start | bytes 393220
  360.1 13.1 %copy-start.12 = (bf16[256,256]{1,0:T(8,128)(2,1)S(1)}, bf16[256,256]{1,0:T(8,128)(2,1)}, u32[]{:S(2)}) copy-start(bf16[256,256]{1,0:T(8,128)(2,1)} %copy-done.11) | copy-start | bytes 393220
  364.8 19.0 %collective-permute-start.6 = (bf16[6,40,512]{2,0,1:T(8,128)(2,1)}, bf16[6,40,512]{2,0,1:T(8,128)(2,1)S(1)}, u32[]{:S(2)}, u32[]{:S(2)}) collective-permute-start(bf16[6,40,512]{2,0,1:T(8,128)(2,1)} %get-tuple-element.190), channel_id=1, source_target_pairs={{0,32},{32,64},{64,96},{96,128},{128,160},{160,192},{192,224},{224... | collective-permute-start | bytes 737288 | tf_op jit(solution)/shard_map/ppermute | solution.py:21
  369.9 13.9 %collective-permute-start.7 = (bf16[6,40,512]{2,0,1:T(8,128)(2,1)}, bf16[6,40,512]{2,0,1:T(8,128)(2,1)S(1)}, u32[]{:S(2)}, u32[]{:S(2)}) collective-permute-start(bf16[6,40,512]{2,0,1:T(8,128)(2,1)} %get-tuple-element.191), channel_id=1, source_target_pairs={{32,0},{64,32},{96,64},{128,96},{160,128},{192,160},{224,192},{256... | collective-permute-start | bytes 737288 | tf_op jit(solution)/shard_map/ppermute | solution.py:22
  385.1 108.8 %copy-start.16 = (f32[256,256]{1,0:T(8,128)S(1)}, f32[256,256]{1,0:T(8,128)}, u32[]{:S(2)}) copy-start(f32[256,256]{1,0:T(8,128)} %copy-done.15) | copy-start | bytes 786436
  385.1 108.8 %copy-start.35 = (bf16[256,768]{1,0:T(8,128)(2,1)S(1)}, bf16[256,768]{1,0:T(8,128)(2,1)}, u32[]{:S(2)}) copy-start(bf16[256,768]{1,0:T(8,128)(2,1)} %param.35) | copy-start | bytes 1179652
  493.3 195.2 %copy-start.1 = (bf16[256,1024]{1,0:T(8,128)(2,1)S(1)}, bf16[256,1024]{1,0:T(8,128)(2,1)}, u32[]{:S(2)}) copy-start(bf16[256,1024]{1,0:T(8,128)(2,1)} %param.38) | copy-start | bytes 1572868
  681.6 6.0 copy-start.14
  (4 other events, 3.0 us)
Sparse Core Ops, SparseCore 0:
  386.8 294.7 all-reduce.6
where the time goes:
time: 707 us; the launch traced here: 696 us
  local copies, waits for them, and re-layouts  249 us (35%)
  waiting for transfers between devices  211 us (30%)
  blocking collectives  107 us (15%)
  matrix products  58.8 us (8%)
  other arithmetic  31.2 us (4%)
  starting transfers between devices  23.1 us (3%)
  between operations  15.2 us (2%)
    psum x1, waiting for transfers between devices, on_device(): lax.psum((local_qkv, local_proj, local_up, local_down, local_gain_attn, l...  187 us
    psum x1, blocking collectives, on_device(): lax.psum((local_qkv, local_proj, local_up, local_down, local_gain_attn, l...  107 us
    reshape x4, local copies, waits for them, and re-layouts, band_strips(): strips.reshape(rows, span * padded.shape[1], heads, padded.shape[2] // he...  80.1 us
    unnamed x112, local copies, waits for them, and re-layouts  33.7 us
    another operation x28, local copies, waits for them, and re-layouts, row_strips(): jnp.stack([lax.slice_in_dim(padded, offset, offset + rows, axis=0) for of...  29 us
    scatter-add x12, local copies, waits for them, and re-layouts, unstrip(): total = total.at[offset:offset + rows].add(strip_sum[:, offset])  25.4 us
    transpose x1, local copies, waits for them, and re-layouts, on_device(): jnp.einsum('ihcn,ichd->inhd', probs_bf, d_attended4, preferred_element_ty...  20.3 us
    transpose x1, local copies, waits for them, and re-layouts, on_device(): jnp.einsum('ihcn,ichd->inhd', d_scores, queries4, preferred_element_type=...  20.3 us
  transfers between devices with their start and end apart: 9, of which 6 were waited for; matrix products, arithmetic and copies ran while one was open for 1% of the time, Pallas kernels for 0%

commit v1 on v0

--- a/solution.py
+++ b/solution.py
@@ -181,8 +181,10 @@
     local_qkv = contract_rows(flat, d_projected)
     grad_frame = (d_mid + contract_cols(d_projected, weight_qkv)).astype(jnp.bfloat16)
     sum_qkv, sum_proj, sum_up, sum_down, sum_gain_attn, sum_gain_mlp = lax.psum(
-        (local_qkv, local_proj, local_up, local_down, local_gain_attn, local_gain_mlp),
-        ("lat", "lon"),
+        lax.psum(
+            (local_qkv, local_proj, local_up, local_down, local_gain_attn, local_gain_mlp), "lon"
+        ),
+        "lat",
     )
     return (
         block_out.reshape(lat_rows, lon_cols, width),

time: 707 us -> 854 us (1.21)
  the two profiles are of different devices: /device:TPU:17 before, /device:TPU:8 now
where the time goes in v1:
time: 854 us; the launch traced here: 842 us
  waiting for transfers between devices  361 us (42%)
  local copies, waits for them, and re-layouts  249 us (29%)
  blocking collectives  99.7 us (12%)
  matrix products  58.8 us (7%)
  other arithmetic  31.2 us (4%)
  starting transfers between devices  26.4 us (3%)
  between operations  15.2 us (2%)
    psum x1, waiting for transfers between devices, on_device(): lax.psum((local_qkv, local_proj, local_up, local_down, local_gain_attn, l...  244 us
    psum x1, waiting for transfers between devices, on_device(): lax.psum(lax.psum((local_qkv, local_proj, local_up, local_down, local_gai...  95.5 us
    reshape x4, local copies, waits for them, and re-layouts, band_strips(): strips.reshape(rows, span * padded.shape[1], heads, padded.shape[2] // he...  80.1 us
    psum x1, blocking collectives, on_device(): lax.psum((local_qkv, local_proj, local_up, local_down, local_gain_attn, l...  55.8 us
    psum x1, blocking collectives, on_device(): lax.psum(lax.psum((local_qkv, local_proj, local_up, local_down, local_gai...  43.9 us
    unnamed x112, local copies, waits for them, and re-layouts  33.7 us
    another operation x28, local copies, waits for them, and re-layouts, row_strips(): jnp.stack([lax.slice_in_dim(padded, offset, offset + rows, axis=0) for of...  29 us
    scatter-add x12, local copies, waits for them, and re-layouts, unstrip(): total = total.at[offset:offset + rows].add(strip_sum[:, offset])  25.4 us
  transfers between devices with their start and end apart: 10, of which 7 were waited for; matrix products, arithmetic and copies ran while one was open for 1% of the time, Pallas kernels for 0%

profile of v1, /device:TPU:8, one launch (start us, length us, event | category | flops | bytes accessed | tf_op | source)
XLA Modules:
  0.0 842.1 jit_solution(11914777226929716620)
XLA Ops:
  8.7 1.9 collective-permute-start
  10.6 4.5 collective-permute-start.1
  15.9 1.7 collective-permute-done.1
  17.8 4.9 collective-permute-start.2
  24.7 2.8 collective-permute-done.2
  27.6 5.6 collective-permute-done.3
  34.4 2.1 fusion.75
  39.3 1.7 stack.109
  47.8 1.7 stack.104
  52.9 1.7 stack.101
  56.3 1.7 stack.99
  64.9 1.8 constant_dynamic-update-slice_fusion.25
  80.3 18.8 %copy.50 = bf16[16,13,28,256]{2,1,3,0:T(8,128)(2,1)} copy(bf16[16,13,28,256]{3,2,0,1:T(8,128)(2,1)} %constant_dynamic-update-slice_fusion.13) | data formatting | bytes 5963776 | tf_op jit(solution)/shard_map/reshape | solution.py:83
  99.1 21.2 %reshape.626 = bf16[16,364,8,32]{1,3,2,0:T(8,128)(2,1)} reshape(bf16[16,13,28,256]{2,1,3,0:T(8,128)(2,1)} %copy.50) | data formatting | bytes 5963776 | tf_op jit(solution)/shard_map/reshape | solution.py:83
  129.0 18.8 %copy.49 = bf16[16,13,28,256]{2,1,3,0:T(8,128)(2,1)} copy(bf16[16,13,28,256]{3,2,0,1:T(8,128)(2,1)} %constant_dynamic-update-slice_fusion) | data formatting | bytes 5963776 | tf_op jit(solution)/shard_map/reshape | solution.py:83
  147.8 21.2 %reshape.625 = bf16[16,364,8,32]{1,3,2,0:T(8,128)(2,1)} reshape(bf16[16,13,28,256]{2,1,3,0:T(8,128)(2,1)} %copy.49) | data formatting | bytes 5963776 | tf_op jit(solution)/shard_map/reshape | solution.py:83
  169.0 2.6 fusion.52
  171.7 3.8 fusion.78
  182.4 4.3 fusion.49
  186.7 17.5 %fusion.20 = bf16[16,16,8,32]{3,1,2,0:T(8,128)(2,1)} fusion(bf16[16,364,8,32]{1,3,2,0:T(8,128)(2,1)} %reshape.626, f32[16,8,16,364]{3,2,1,0:T(8,128)} %fusion.49, f32[16,8,16,364]{3,2,1,0:T(8,128)} %copy-done.5, f32[16,8,16]{2,1,0:T(8,128)S(1)} %get-tuple-element.232), kind=kOutput, calls=%fused_computation.27 | convolution fusion | flops 52996460 | bytes 9084928 | tf_op jit(solution)/shard_map/ihcn,inhd->ichd/dot_general | solution.py:161
  204.2 17.6 %convolution_bitcast_fusion.1 = f32[16,364,8,32]{1,3,2,0:T(8,128)} fusion(f32[16,8,16,364]{3,2,1,0:T(8,128)} %fusion.49, bf16[16,16,8,32]{3,2,1,0:T(8,128)(2,1)S(1)} %reshape.602, f32[16,8,16,364]{3,2,1,0:T(8,128)} %copy-done.5, f32[16,8,16]{2,1,0:T(8,128)S(1)} %get-tuple-element.232), kind=kOutput, calls=%fused_computation.8 | convolution fusion | flops 52930924 | bytes 12066816 | tf_op jit(solution)/shard_map/ihcn,ichd->inhd/dot_general | solution.py:164
  221.8 5.6 convolution_bitcast_fusion
  227.4 20.3 %copy.46 = f32[16,364,8,32]{3,2,0,1:T(8,128)} copy(f32[16,364,8,32]{1,3,2,0:T(8,128)} %convolution_bitcast_fusion) | data formatting | bytes 11927552 | tf_op jit(solution)/shard_map/ihcn,ichd->inhd/transpose | solution.py:167
  247.7 16.9 %reshape.609 = f32[16,13,28,256]{3,0,2,1:T(8,128)} reshape(f32[16,364,8,32]{3,2,0,1:T(8,128)} %copy.46) | data formatting | bytes 11927552 | tf_op jit(solution)/shard_map/reshape | solution.py:169
  264.6 20.3 %copy.44 = f32[16,364,8,32]{3,2,0,1:T(8,128)} copy(f32[16,364,8,32]{1,3,2,0:T(8,128)} %convolution_bitcast_fusion.1) | data formatting | bytes 11927552 | tf_op jit(solution)/shard_map/ihcn,ichd->inhd/transpose | solution.py:164
  285.0 16.8 %reshape.608 = f32[16,13,28,256]{3,0,2,1:T(8,128)} reshape(f32[16,364,8,32]{3,2,0,1:T(8,128)} %copy.44) | data formatting | bytes 11927552 | tf_op jit(solution)/shard_map/reshape | solution.py:166
  301.8 3.8 constant_dynamic-update-slice_fusion.27
  308.2 4.1 copy-done.2
  312.4 2.2 scatter-add.45
  316.1 2.2 scatter-add.46
  319.7 2.2 scatter-add.49
  323.3 2.2 scatter-add.50
  327.0 2.2 scatter-add.51
  330.6 2.2 scatter-add.54
  334.2 2.2 scatter-add.55
  339.3 2.5 scatter-add.59
  343.2 2.5 scatter-add.60
  347.1 2.5 scatter-add.61
  351.0 2.5 scatter-add.64
  353.7 2.1 collective-permute-start.4
  355.8 4.7 collective-permute-start.5
  364.6 5.4 collective-permute-start.6
  374.2 10.2 %collective-permute-done.6 = bf16[6,40,512]{2,0,1:T(8,128)(2,1)S(1)} collective-permute-done((bf16[6,40,512]{2,0,1:T(8,128)(2,1)}, bf16[6,40,512]{2,0,1:T(8,128)(2,1)S(1)}, u32[]{:S(2)}, u32[]{:S(2)}) %collective-permute-start.6) | collective-permute-done | bytes 245792 | tf_op jit(solution)/shard_map/ppermute | solution.py:21
  387.4 244.0 %all-reduce.10.cloned.1.call-done = (f32[256,768]{0,1:T(8,128)}, f32[256,256]{1,0:T(8,128)}, f32[256,1024]{1,0:T(8,128)}, f32[1024,256]{1,0:T(8,128)}) async-done(((f32[256,768]{0,1:T(8,128)}, f32[256,256]{1,0:T(8,128)}, f32[256,1024]{1,0:T(8,128)}, f32[1024,256]{1,0:T(8,128)}), (f32[256,768]{0,1:T(8,128)}, f32[256,256]{1,0:T(8,128)}, f32[256,1024]{1,0:T(8,128)}, ...) | async-done | bytes 3145744 | tf_op jit(solution)/shard_map/psum | solution.py:184
  631.4 55.8 %all-reduce.3 = (f32[256]{0:T(256)S(1)}, f32[256]{0:T(256)S(1)}) all-reduce(f32[256]{0:T(256)S(1)} %get-tuple-element.180, f32[256]{0:T(256)S(1)} %get-tuple-element.182), channel_id=1, replica_groups=mesh['lat'=16,'lon'=32] {'lon'}, use_global_device_ids=true, to_apply=%region_16.17 | all-reduce | flops 512 | bytes 4096 | tf_op jit(solution)/shard_map/psum | solution.py:184
  687.2 43.9 %all-reduce.5 = (f32[256]{0:T(256)S(1)}, f32[256]{0:T(256)S(1)}) all-reduce(f32[256]{0:T(256)S(1)} %get-tuple-element.184, f32[256]{0:T(256)S(1)} %get-tuple-element.185), channel_id=1, replica_groups=mesh['lat'=16,'lon'=32] {'lat'}, use_global_device_ids=true, to_apply=%region_17.18 | all-reduce | flops 512 | bytes 4096 | tf_op jit(solution)/shard_map/psum | solution.py:183
  732.7 95.5 %all-reduce.12.cloned.1.call-done = (f32[256,768]{0,1:T(8,128)}, f32[256,256]{1,0:T(8,128)}, f32[256,1024]{1,0:T(8,128)}, f32[1024,256]{1,0:T(8,128)}) async-done(((f32[256,768]{0,1:T(8,128)}, f32[256,256]{1,0:T(8,128)}, f32[256,1024]{1,0:T(8,128)}, f32[1024,256]{1,0:T(8,128)}), (f32[256,768]{0,1:T(8,128)}, f32[256,256]{1,0:T(8,128)}, f32[256,1024]{1,0:T(8,128)}, ...) | async-done | bytes 3145744 | tf_op jit(solution)/shard_map/psum | solution.py:183
  832.0 2.1 multiply_convert_fusion.2
  (214 shorter events, 92.1 us)
Async XLA Ops:
  7.2 170.9 %copy-start = (bf16[256,1024]{1,0:T(8,128)(2,1)S(1)}, bf16[256,1024]{1,0:T(8,128)(2,1)}, u32[]{:S(2)}) copy-start(bf16[256,1024]{1,0:T(8,128)(2,1)} %param.38) | copy-start | bytes 1572868
  7.2 624.2 %all-reduce.10.cloned.1.call-start = ((), (), s32[]{:S(2)}) async-start(), calls=%async_computation | async-start | bytes 6291456 | tf_op jit(solution)/shard_map/psum | solution.py:184
  8.7 7.2 collective-permute-start
  10.6 7.0 collective-permute-start.1
  17.8 9.8 %collective-permute-start.2 = (bf16[6,28,512]{2,1,0:T(8,128)(2,1)S(1)}, bf16[6,28,512]{2,1,0:T(8,128)(2,1)S(1)}, u32[]{:S(2)}, u32[]{:S(2)}) collective-permute-start(bf16[6,28,512]{2,1,0:T(8,128)(2,1)S(1)} %get-tuple-element.226), channel_id=1, source_target_pairs={{0,32},{32,64},{64,96},{96,128},{128,160},{160,192},{192,224},{224... | collective-permute-start | bytes 516104 | tf_op jit(solution)/shard_map/ppermute | solution.py:21
  22.7 10.5 %collective-permute-start.3 = (bf16[6,28,512]{2,1,0:T(8,128)(2,1)S(1)}, bf16[6,28,512]{2,1,0:T(8,128)(2,1)S(1)}, u32[]{:S(2)}, u32[]{:S(2)}) collective-permute-start(bf16[6,28,512]{2,1,0:T(8,128)(2,1)S(1)} %get-tuple-element.227), channel_id=1, source_target_pairs={{32,0},{64,32},{96,64},{128,96},{160,128},{192,160},{224,192},{256... | collective-permute-start | bytes 516104 | tf_op jit(solution)/shard_map/ppermute | solution.py:22
  38.6 19.4 %copy-start.31 = (bf16[448,256]{1,0:T(8,128)(2,1)S(1)}, bf16[448,256]{1,0:T(8,128)(2,1)}, u32[]{:S(2)}) copy-start(bf16[448,256]{1,0:T(8,128)(2,1)} %get-tuple-element.212) | copy-start | bytes 688132
  38.6 20.1 %copy-start.30 = (bf16[448,256]{1,0:T(8,128)(2,1)S(1)}, bf16[448,256]{1,0:T(8,128)(2,1)}, u32[]{:S(2)}) copy-start(bf16[448,256]{1,0:T(8,128)(2,1)} %get-tuple-element.213) | copy-start | bytes 688132
  39.3 19.4 %copy-start.29 = (bf16[448,256]{1,0:T(8,128)(2,1)S(1)}, bf16[448,256]{1,0:T(8,128)(2,1)}, u32[]{:S(2)}) copy-start(bf16[448,256]{1,0:T(8,128)(2,1)} %get-tuple-element.214) | copy-start | bytes 688132
  64.9 10.2 %copy-start.26 = (bf16[16,1,28,256]{3,2,0,1:T(8,128)(2,1)S(1)}, bf16[16,1,28,256]{3,2,0,1:T(8,128)(2,1)}, u32[]{:S(2)}) copy-start(bf16[16,1,28,256]{3,2,0,1:T(8,128)(2,1)} %stack.104) | copy-start | bytes 688132
  64.9 10.9 %copy-start.25 = (bf16[16,1,28,256]{3,2,0,1:T(8,128)(2,1)S(1)}, bf16[16,1,28,256]{3,2,0,1:T(8,128)(2,1)}, u32[]{:S(2)}) copy-start(bf16[16,1,28,256]{3,2,0,1:T(8,128)(2,1)} %stack.105) | copy-start | bytes 688132
  64.9 11.7 %copy-start.24 = (bf16[16,1,28,256]{3,2,0,1:T(8,128)(2,1)S(1)}, bf16[16,1,28,256]{3,2,0,1:T(8,128)(2,1)}, u32[]{:S(2)}) copy-start(bf16[16,1,28,256]{3,2,0,1:T(8,128)(2,1)} %stack.106) | copy-start | bytes 688132
  64.9 12.4 %copy-start.23 = (bf16[16,1,28,256]{3,2,0,1:T(8,128)(2,1)S(1)}, bf16[16,1,28,256]{3,2,0,1:T(8,128)(2,1)}, u32[]{:S(2)}) copy-start(bf16[16,1,28,256]{3,2,0,1:T(8,128)(2,1)} %stack.107) | copy-start | bytes 688132
  64.9 13.1 %copy-start.21 = (bf16[16,1,28,256]{3,2,0,1:T(8,128)(2,1)S(1)}, bf16[16,1,28,256]{3,2,0,1:T(8,128)(2,1)}, u32[]{:S(2)}) copy-start(bf16[16,1,28,256]{3,2,0,1:T(8,128)(2,1)} %stack.108) | copy-start | bytes 688132
  64.9 13.9 %copy-start.19 = (bf16[16,1,28,256]{3,2,0,1:T(8,128)(2,1)S(1)}, bf16[16,1,28,256]{3,2,0,1:T(8,128)(2,1)}, u32[]{:S(2)}) copy-start(bf16[16,1,28,256]{3,2,0,1:T(8,128)(2,1)} %stack.109) | copy-start | bytes 688132
  64.9 14.6 %copy-start.17 = (bf16[16,1,28,256]{3,2,0,1:T(8,128)(2,1)S(1)}, bf16[16,1,28,256]{3,2,0,1:T(8,128)(2,1)}, u32[]{:S(2)}) copy-start(bf16[16,1,28,256]{3,2,0,1:T(8,128)(2,1)} %stack.110) | copy-start | bytes 688132
  120.3 4.3 copy-start.22
  120.3 5.1 copy-start.20
  120.3 5.8 copy-start.18
  169.0 2.6 copy-start.38
  171.7 3.8 copy-start.4
  175.5 1.6 copy-start.5
  175.5 2.1 copy-start.34
  175.5 2.4 copy-start.8
  175.5 2.4 copy-start.39
  177.1 1.3 copy-start.42
  177.2 1.7 copy-start.13
  177.3 1.7 copy-start.40
  177.6 1.5 copy-start.11
  178.4 2.4 copy-start.27
  182.0 4.7 copy-start.9
  301.8 4.4 copy-start.3
  307.8 4.4 copy-start.2
  353.5 7.0 copy-start.28
  353.5 7.0 copy-start.37
  353.7 17.8 %copy-start.7 = (bf16[256,1024]{1,0:T(8,128)(2,1)S(1)}, bf16[256,1024]{1,0:T(8,128)(2,1)}, u32[]{:S(2)}) copy-start(bf16[256,1024]{1,0:T(8,128)(2,1)} %copy-done.6) | copy-start | bytes 1572868
  353.7 8.4 collective-permute-start.4
  355.8 17.0 %copy-start.33 = (bf16[16,16,8,32]{3,1,2,0:T(8,128)(2,1)S(1)}, bf16[16,16,8,32]{3,1,2,0:T(8,128)(2,1)}, u32[]{:S(2)}) copy-start(bf16[16,16,8,32]{3,1,2,0:T(8,128)(2,1)} %fusion.20) | copy-start | bytes 393220
  355.8 7.8 collective-permute-start.5
  362.1 11.2 %copy-start.10 = (bf16[256,256]{1,0:T(8,128)(2,1)S(1)}, bf16[256,256]{1,0:T(8,128)(2,1)}, u32[]{:S(2)}) copy-start(bf16[256,256]{1,0:T(8,128)(2,1)} %copy-done.9) | copy-start | bytes 393220
  362.1 11.2 %copy-start.12 = (bf16[256,256]{1,0:T(8,128)(2,1)S(1)}, bf16[256,256]{1,0:T(8,128)(2,1)}, u32[]{:S(2)}) copy-start(bf16[256,256]{1,0:T(8,128)(2,1)} %copy-done.11) | copy-start | bytes 393220
  364.6 19.9 %collective-permute-start.6 = (bf16[6,40,512]{2,0,1:T(8,128)(2,1)}, bf16[6,40,512]{2,0,1:T(8,128)(2,1)S(1)}, u32[]{:S(2)}, u32[]{:S(2)}) collective-permute-start(bf16[6,40,512]{2,0,1:T(8,128)(2,1)} %get-tuple-element.196), channel_id=1, source_target_pairs={{0,32},{32,64},{64,96},{96,128},{128,160},{160,192},{192,224},{224... | collective-permute-start | bytes 737288 | tf_op jit(solution)/shard_map/ppermute | solution.py:21
  370.0 14.5 %collective-permute-start.7 = (bf16[6,40,512]{2,0,1:T(8,128)(2,1)}, bf16[6,40,512]{2,0,1:T(8,128)(2,1)S(1)}, u32[]{:S(2)}, u32[]{:S(2)}) collective-permute-start(bf16[6,40,512]{2,0,1:T(8,128)(2,1)} %get-tuple-element.197), channel_id=1, source_target_pairs={{32,0},{64,32},{96,64},{128,96},{160,128},{192,160},{224,192},{256... | collective-permute-start | bytes 737288 | tf_op jit(solution)/shard_map/ppermute | solution.py:22
  387.3 344.4 %copy-start.16 = (f32[256,256]{1,0:T(8,128)S(1)}, f32[256,256]{1,0:T(8,128)}, u32[]{:S(2)}) copy-start(f32[256,256]{1,0:T(8,128)} %copy-done.15) | copy-start | bytes 786436
  387.3 344.4 %copy-start.35 = (bf16[256,768]{1,0:T(8,128)(2,1)S(1)}, bf16[256,768]{1,0:T(8,128)(2,1)}, u32[]{:S(2)}) copy-start(bf16[256,768]{1,0:T(8,128)(2,1)} %param.35) | copy-start | bytes 1179652
  387.4 440.8 %all-reduce.12.cloned.1.call-start = ((), (), s32[]{:S(2)}) async-start(), calls=%async_computation.1 | async-start | bytes 6291456 | tf_op jit(solution)/shard_map/psum | solution.py:183
  731.2 103.9 %copy-start.1 = (bf16[256,1024]{1,0:T(8,128)(2,1)S(1)}, bf16[256,1024]{1,0:T(8,128)(2,1)}, u32[]{:S(2)}) copy-start(bf16[256,1024]{1,0:T(8,128)(2,1)} %param.38) | copy-start | bytes 1572868
  828.2 6.0 copy-start.14
  (5 other events, 4.0 us)
Sparse Core Ops, SparseCore 0:
  387.5 243.8 all-reduce.9
  634.6 193.5 all-reduce.11
